TPU v7x, 256 devices: a whole 4x4x8 slice. The times are simulated.
256 devices in a mesh: prow: 8 (over z_lo, y), pcol: 32 (over z_hi, x, core).
Axes of the slice: x: 4, y: 4, z: 8 (z_hi: 4, z_lo: 2; z = z_hi * 2 + z_lo), core: 2. Of those that a mesh axis runs over, the one named last changes fastest.
Arguments:
- ancestor_inverse: bfloat16 [24576, 24576], P('prow', 'pcol'), may hold values from -6 to 6
- tile_pattern: int32 [64, 64], replicated, may hold values 0 or 1
- rows_first: int32 [24576], replicated, may hold values 0 or 1
- rows_second: int32 [24576], replicated, may hold values 0 or 1
- panel_first: bfloat16 [24576, 512], P('prow', 'pcol'), may hold values from -0.0390625 to 0.0390625
- panel_second: bfloat16 [24576, 512], P('prow', 'pcol'), may hold values from -0.21875 to 0.21875
- inner_panel: bfloat16 [512, 512], replicated, may hold values from -0.25 to 0.25
- pivot_first: float32 [512, 512], replicated, may hold values from -6 to 6
- pivot_second: float32 [512, 512], replicated, may hold values from -6 to 6
Outputs:
- column_first: bfloat16 [24576, 512], P(('prow', 'pcol'))
- diagonal_first: float32 [512, 512], replicated
- inner_second: float32 [512, 512], replicated
- column_second: bfloat16 [24576, 512], P(('prow', 'pcol'))
- diagonal_second: float32 [512, 512], replicated
Inputs may be any that keep to these rules, and one draw needn't show every extreme that they name: `tile_pattern`: 1 marks a structurally nonzero tile. `rows_first`: 1 marks a row of the first supernode's structure. By construction here, a row belongs to the second supernode's structure only where both rows_second and rows_first are 1.
All inputs are finite; a program needn't handle non-finite values.
Results may differ from a plain program's by a relative error of at most 0.015.
Values may be sent and summed in bfloat16 or wider, within the bound.
A program may use at most 128 MiB of HBM per device.

v0:
```python
import jax
import jax.numpy as jnp
from jax import lax
from jax.sharding import PartitionSpec as P

TILE = 384


def from_root(shard, axis, root):
    mine = lax.axis_index(axis) == root
    return lax.psum(jnp.where(mine, shard, jnp.zeros_like(shard)), axis)


def mask_tiles(block, pattern, row_start, col_start):
    tile_rows = block.shape[0] // TILE
    tile_cols = block.shape[1] // TILE
    window = lax.dynamic_slice(pattern, (row_start, col_start), (tile_rows, tile_cols)).astype(
        jnp.bfloat16
    )
    shaped = block.reshape(tile_rows, TILE, tile_cols, TILE) * window[:, None, :, None]
    return shaped.reshape(block.shape)


def body(
    ancestor_inverse,
    tile_pattern,
    rows_first,
    rows_second,
    panel_first,
    panel_second,
    inner_panel,
    pivot_first,
    pivot_second,
):
    row_count = lax.axis_size("prow")
    col_count = lax.axis_size("pcol")
    row_id = lax.axis_index("prow")
    col_id = lax.axis_index("pcol")
    row_block = ancestor_inverse.shape[0]
    col_block = ancestor_inverse.shape[1]
    share = row_block // col_count
    sparse = mask_tiles(
        ancestor_inverse, tile_pattern, row_id * (row_block // TILE), col_id * (col_block // TILE)
    )
    struct_first = lax.dynamic_slice_in_dim(rows_first, row_id * row_block, row_block).astype(
        jnp.bfloat16
    )
    struct_second = struct_first * lax.dynamic_slice_in_dim(
        rows_second, row_id * row_block, row_block
    ).astype(jnp.bfloat16)
    local_first = panel_first * struct_first[:, None]
    local_second = panel_second * struct_second[:, None]
    source = col_id * row_count // col_count
    offset = col_id * col_block - source * row_block

    def summed_terms(columns):
        return jnp.dot(sparse, columns, preferred_element_type=jnp.float32)

    def ancestor_terms(local):
        full = lax.all_gather(local, "pcol", axis=1, tiled=True)
        mirrored = from_root(lax.dynamic_slice_in_dim(full, offset, col_block, 0), "prow", source)
        return (
            full,
            lax.psum_scatter(
                summed_terms(mirrored).astype(jnp.bfloat16), "pcol", scatter_dimension=0, tiled=True
            ).astype(jnp.float32),
        )

    full_first, sum_first = ancestor_terms(local_first)
    full_second, sum_second = ancestor_terms(local_second)
    column_first = (-sum_first).astype(jnp.bfloat16)
    own_first = lax.dynamic_slice_in_dim(full_first, col_id * share, share, 0)
    own_second = lax.dynamic_slice_in_dim(full_second, col_id * share, share, 0)
    corr_first, crossed = lax.psum(
        (
            jnp.dot(own_first.T, column_first, preferred_element_type=jnp.float32),
            jnp.dot(column_first.T, own_second, preferred_element_type=jnp.float32),
        ),
        ("prow", "pcol"),
    )
    diagonal_first = pivot_first - corr_first
    column_second = (
        -(sum_second + jnp.dot(column_first, inner_panel, preferred_element_type=jnp.float32))
    ).astype(jnp.bfloat16)
    inner_wide = inner_panel.astype(jnp.float32)
    inner_second = -(jnp.dot(diagonal_first, inner_wide, precision=lax.Precision.HIGHEST) + crossed)
    corr_second = lax.psum(
        jnp.dot(own_second.T, column_second, preferred_element_type=jnp.float32), ("prow", "pcol")
    )
    diagonal_second = (
        pivot_second
        - jnp.dot(inner_wide.T, inner_second, precision=lax.Precision.HIGHEST)
        - corr_second
    )
    return (column_first, diagonal_first, inner_second, column_second, diagonal_second)


def solution(mesh):
    return jax.shard_map(
        body,
        mesh=mesh,
        in_specs=(
            P("prow", "pcol"),
            P(),
            P(),
            P(),
            P("prow", "pcol"),
            P("prow", "pcol"),
            P(),
            P(),
            P(),
        ),
        out_specs=(P(("prow", "pcol"), None), P(), P(), P(("prow", "pcol"), None), P()),
        check_vma=False,
    )
```

profile of v0, /device:TPU:8, one launch (start us, length us, event | category | flops | bytes accessed | tf_op | source)
XLA Modules:
  0.0 701.2 jit_solution(2915164507721282915)
XLA Ops:
  7.2 0.0 copy-start
  7.2 0.0 all-gather.5.cloned.1.call-start
  7.2 0.8 fusion.13
  8.0 1.5 broadcast_multiply_fusion
  9.6 0.0 all-gather.5.cloned.1.call-update
  9.6 0.0 all-gather.3.cloned.1.call-start
  9.6 1.5 broadcast_multiply_fusion.1
  11.2 0.0 all-gather.3.cloned.1.call-update
  11.2 0.0 all-reduce.7.cloned.1.call-start
  11.3 59.7 %all-gather.5.cloned.1.call-done = bf16[3072,512]{0,1:T(8,128)(2,1)} async-done(((bf16[3072,16]{0,1:T(8,128)(2,1)}), bf16[3072,512]{0,1:T(8,128)(2,1)}) %all-gather.5.cloned.1.call-update) | async-done | bytes 3145744 | tf_op jit(solution)/shard_map/all_gather | solution.py:60
  71.0 2.1 dynamic-slice_select_fusion
  73.2 55.8 %all-gather.3.cloned.1.call-done = bf16[3072,512]{0,1:T(8,128)(2,1)} async-done(((bf16[3072,16]{0,1:T(8,128)(2,1)}), bf16[3072,512]{0,1:T(8,128)(2,1)}) %all-gather.3.cloned.1.call-update) | async-done | bytes 3145744 | tf_op jit(solution)/shard_map/all_gather | solution.py:60
  129.0 2.1 dynamic-slice_select_fusion.1
  131.1 0.0 all-reduce.7.cloned.1.call-update
  131.2 0.0 reduce-scatter.3.cloned.1.call-start
  131.2 0.8 dynamic-slice_convert_fusion.2
  132.0 2.5 mul.55
  134.5 3.0 copy.18
  137.5 76.0 %all-reduce.7.cloned.1.call-done = (bf16[768,512]{0,1:T(8,128)(2,1)}, bf16[768,512]{0,1:T(8,128)(2,1)}) async-done(((bf16[768,512]{0,1:T(8,128)(2,1)}, bf16[768,512]{0,1:T(8,128)(2,1)}), (bf16[768,512]{0,1:T(8,128)(2,1)}, bf16[768,512]{0,1:T(8,128)(2,1)})) %all-reduce.7.cloned.1.call-update) | async-done | bytes 1572880 | tf_op jit(solution)/shard_map/psum | solution.py:11
  213.4 0.0 copy-start.9
  213.4 8.4 %convolution_convert_fusion.1 = bf16[3072,512]{1,0:T(8,128)(2,1)} fusion(bf16[768,512]{0,1:T(8,128)(2,1)} %get-tuple-element.13, bf16[3072,768]{1,0:T(8,128)(2,1)} %param.9, bf16[3072,768]{1,0:T(8,128)(2,1)} %bitcast.21), kind=kOutput, calls=%fused_computation.1 | convolution fusion | flops 2419851264 | bytes 13369344 | tf_op jit(solution)/shard_map/dot_general | solution.py:57
  221.8 0.0 reduce-scatter.3.cloned.1.call-update
  221.8 0.0 reduce-scatter.5.cloned.1.call-start
  221.9 0.0 copy-done.9
  221.9 7.9 %convolution_convert_fusion = bf16[3072,512]{1,0:T(8,128)(2,1)} fusion(bf16[768,512]{0,1:T(8,128)(2,1)S(1)} %copy-done.9, bf16[3072,768]{1,0:T(8,128)(2,1)} %param.9, bf16[3072,768]{1,0:T(8,128)(2,1)} %bitcast.22), kind=kOutput, calls=%fused_computation | convolution fusion | flops 2419851264 | bytes 13369344 | tf_op jit(solution)/shard_map/dot_general | solution.py:57
  229.8 0.0 reduce-scatter.5.cloned.1.call-update
  229.8 0.0 copy-start.6
  229.8 0.2 all-reduce.5.cloned.1.call-start
  230.0 88.8 %reduce-scatter.3.cloned.1.call-done = bf16[96,512]{1,0:T(8,128)(2,1)} async-done(((bf16[3072,512]{1,0:T(8,128)(2,1)}), bf16[96,512]{1,0:T(8,128)(2,1)}) %reduce-scatter.3.cloned.1.call-update) | async-done | bytes 98320 | tf_op jit(solution)/shard_map/reduce_scatter | solution.py:64
  318.8 0.9 negate_convert_fusion
  319.8 0.0 copy-start.4
  319.8 0.0 copy-start.5
  319.8 2.4 fusion.11
  322.2 2.3 fusion.7
  324.4 91.8 %reduce-scatter.5.cloned.1.call-done = bf16[96,512]{1,0:T(8,128)(2,1)} async-done(((bf16[3072,512]{1,0:T(8,128)(2,1)}), bf16[96,512]{1,0:T(8,128)(2,1)}) %reduce-scatter.5.cloned.1.call-update) | async-done | bytes 98320 | tf_op jit(solution)/shard_map/reduce_scatter | solution.py:64
  416.3 0.0 copy-done
  416.3 1.1 fusion.6
  417.4 0.0 copy-start.8
  417.4 2.4 fusion.9
  419.8 0.0 all-reduce.5.cloned.1.call-update
  419.8 0.0 copy-done.6
  419.8 1.3 copy.14
  421.1 0.0 copy-done.4
  421.1 264.4 %all-reduce.5.cloned.1.call-done = (f32[512,512]{1,0:T(8,128)}, f32[512,512]{1,0:T(8,128)}, f32[512,512]{0,1:T(8,128)}) async-done(((f32[512,512]{1,0:T(8,128)}, f32[512,512]{1,0:T(8,128)}, f32[512,512]{0,1:T(8,128)}), (f32[512,512]{1,0:T(8,128)}, f32[512,512]{1,0:T(8,128)}, f32[512,512]{0,1:T(8,128)})) %all-reduce.5.cloned.1.call-update) | async-done | bytes 3145744 | tf_op jit(solution)/shard_map/psum | solution.py:74
  685.6 0.0 copy-start.3
  685.6 0.0 copy-start.7
  685.6 0.0 copy-done.5
  685.6 1.6 sub.18
  687.2 0.0 copy-done.8
  687.2 0.0 copy-start.1
  687.2 2.6 fusion.2
  689.8 0.0 copy-start.2
  689.8 0.0 copy-done.3
  689.8 0.0 copy-done.7
  689.8 2.0 fusion.4
  691.8 2.5 copy.16
  694.4 0.0 copy-done.1
  694.4 0.0 copy-done.2
Async XLA Ops:
  7.2 409.1 %copy-start = (bf16[512,512]{1,0:T(8,128)(2,1)S(1)}, bf16[512,512]{1,0:T(8,128)(2,1)}, u32[]{:S(2)}) copy-start(bf16[512,512]{1,0:T(8,128)(2,1)} %param.15) | copy-start | bytes 1572868
  7.2 63.8 %all-gather.5.cloned.1.call-start = ((), (), s32[]{:S(2)}) async-start(), calls=%async_computation.4 | async-start | bytes 3244032 | tf_op jit(solution)/shard_map/all_gather | solution.py:60
  9.6 119.4 %all-gather.3.cloned.1.call-start = ((), (), s32[]{:S(2)}) async-start(), calls=%async_computation.2 | async-start | bytes 3244032 | tf_op jit(solution)/shard_map/all_gather | solution.py:60
  11.2 202.2 %all-reduce.7.cloned.1.call-start = ((), (), s32[]{:S(2)}) async-start(), calls=%async_computation.7 | async-start | bytes 3145728 | tf_op jit(solution)/shard_map/psum | solution.py:11
  131.2 187.7 %reduce-scatter.3.cloned.1.call-start = ((), (), s32[]{:S(2)}) async-start(), calls=%async_computation.3 | async-start | bytes 3244032 | tf_op jit(solution)/shard_map/reduce_scatter | solution.py:64
  213.4 8.4 %copy-start.9 = (bf16[768,512]{0,1:T(8,128)(2,1)S(1)}, bf16[768,512]{0,1:T(8,128)(2,1)}, u32[]{:S(2)}) copy-start(bf16[768,512]{0,1:T(8,128)(2,1)} %get-tuple-element.14) | copy-start | bytes 2359300
  221.8 194.4 %reduce-scatter.5.cloned.1.call-start = ((), (), s32[]{:S(2)}) async-start(), calls=%async_computation.5 | async-start | bytes 3244032 | tf_op jit(solution)/shard_map/reduce_scatter | solution.py:64
  229.8 190.0 %copy-start.6 = (f32[512,512]{1,0:T(8,128)S(1)}, f32[512,512]{1,0:T(8,128)}, u32[]{:S(2)}) copy-start(f32[512,512]{1,0:T(8,128)} %param.17) | copy-start | bytes 3145732
  229.8 455.8 %all-reduce.5.cloned.1.call-start = ((), (), s32[]{:S(2)}) async-start(), calls=%async_computation.6 | async-start | bytes 6291456 | tf_op jit(solution)/shard_map/psum | solution.py:74
  319.8 101.4 %copy-start.4 = (bf16[96,512]{1,0:T(8,128)(2,1)}, bf16[96,512]{1,0:T(8,128)(2,1)S(1)}, u32[]{:S(2)}) copy-start(bf16[96,512]{1,0:T(8,128)(2,1)S(1)} %negate_convert_fusion) | copy-start | bytes 294916
  319.8 365.8 %copy-start.5 = (f32[512,512]{1,0:T(8,128)S(1)}, f32[512,512]{1,0:T(8,128)}, u32[]{:S(2)}) copy-start(f32[512,512]{1,0:T(8,128)} %param.16) | copy-start | bytes 3145732
  417.4 269.8 %copy-start.8 = (bf16[96,512]{1,0:T(8,128)(2,1)}, bf16[96,512]{1,0:T(8,128)(2,1)S(1)}, u32[]{:S(2)}) copy-start(bf16[96,512]{1,0:T(8,128)(2,1)S(1)} %fusion.6) | copy-start | bytes 294916
  685.6 4.2 copy-start.3
  685.6 4.2 copy-start.7
  687.2 7.2 %copy-start.1 = (f32[512,512]{1,0:T(8,128)}, f32[512,512]{1,0:T(8,128)S(1)}, u32[]{:S(2)}) copy-start(f32[512,512]{1,0:T(8,128)S(1)} %sub.18) | copy-start | bytes 3145732
  689.8 4.6 copy-start.2
Sparse Core Ops, SparseCore 0:
  11.1 59.8 all-gather.4
  74.1 54.8 all-gather.2
  132.3 81.1 all-reduce.6
  222.0 96.8 reduce-scatter.2
  323.1 93.1 reduce-scatter.4
  422.5 263.0 all-reduce.4
where the time goes:
time: 702 us; the launch traced here: 701 us
  waiting for transfers between devices  637 us (91%)
  matrix products  29 us (4%)
  between operations  14.3 us (2%)
  other arithmetic  11.4 us (2%)
  local copies, waits for them, and re-layouts  9.39 us (1%)
    psum x1, waiting for transfers between devices, body(): lax.psum((jnp.dot(own_first.T, column_first, preferred_element_type=jnp.f...  264 us
    reduce_scatter x2, waiting for transfers between devices, ancestor_terms(): lax.psum_scatter(summed_terms(mirrored).astype(jnp.bfloat16), 'pcol', sca...  181 us
    all_gather x2, waiting for transfers between devices, ancestor_terms(): full = lax.all_gather(local, 'pcol', axis=1, tiled=True)  116 us
    psum x1, waiting for transfers between devices, from_root(): return lax.psum(jnp.where(mine, shard, jnp.zeros_like(shard)), axis)  76 us
    dot_general x2, matrix products, summed_terms(): return jnp.dot(sparse, columns, preferred_element_type=jnp.float32)  16.2 us
  transfers between devices with their start and end apart: 6, of which 6 were waited for; matrix products, arithmetic and copies ran while one was open for 4% of the time, Pallas kernels for 0%

commit v1 on v0

--- a/solution.py
+++ b/solution.py
@@ -72,11 +72,14 @@
     own_first = lax.dynamic_slice_in_dim(full_first, col_id * share, share, 0)
     own_second = lax.dynamic_slice_in_dim(full_second, col_id * share, share, 0)
     corr_first, crossed = lax.psum(
-        (
-            jnp.dot(own_first.T, column_first, preferred_element_type=jnp.float32),
-            jnp.dot(column_first.T, own_second, preferred_element_type=jnp.float32),
+        lax.psum(
+            (
+                jnp.dot(own_first.T, column_first, preferred_element_type=jnp.float32),
+                jnp.dot(column_first.T, own_second, preferred_element_type=jnp.float32),
+            ),
+            "prow",
         ),
-        ("prow", "pcol"),
+        "pcol",
     )
     diagonal_first = pivot_first - corr_first
     column_second = (

time: 702 us -> 1080 us (1.54)
  waiting for transfers between devices: 637 us -> 1010 us
    psum x0 -> x2, waiting for transfers between devices: none -> 545 us  [the longest x1 287 us: body(): lax.psum(lax.psum((jnp.dot(own_first.T, column_first, preferred_element_t...]
    psum x1, waiting for transfers between devices: 264 us -> 76.3 us  [body(): lax.psum((jnp.dot(own_first.T, column_first, preferred_element_type=jnp.f...]
    reduce_scatter x2, waiting for transfers between devices: 181 us -> 198 us  [ancestor_terms(): lax.psum_scatter(summed_terms(mirrored).astype(jnp.bfloat16), 'pcol', sca...]
  transfers between devices with their start and end apart: 6 -> 8, of which waited for: 6 -> 8; matrix products, arithmetic and copies ran while one was open for 4% -> 2% of each run, Pallas kernels for 0% -> 0%
where the time goes in v1:
time: 1080 us
  waiting for transfers between devices  1010 us (94%)
  matrix products  30.5 us (3%)
  between operations  14.3 us (1%)
  other arithmetic  11.3 us (1%)
    psum x1, waiting for transfers between devices, body(): lax.psum(lax.psum((jnp.dot(own_first.T, column_first, preferred_element_t...  287 us
    psum x1, waiting for transfers between devices, body(): lax.psum(jnp.dot(own_second.T, column_second, preferred_element_type=jnp....  257 us
    reduce_scatter x2, waiting for transfers between devices, ancestor_terms(): lax.psum_scatter(summed_terms(mirrored).astype(jnp.bfloat16), 'pcol', sca...  198 us
    all_gather x2, waiting for transfers between devices, ancestor_terms(): full = lax.all_gather(local, 'pcol', axis=1, tiled=True)  116 us
    psum x1, waiting for transfers between devices, body(): lax.psum((jnp.dot(own_first.T, column_first, preferred_element_type=jnp.f...  76.3 us
    psum x1, waiting for transfers between devices, from_root(): return lax.psum(jnp.where(mine, shard, jnp.zeros_like(shard)), axis)  76 us
  transfers between devices with their start and end apart: 8, of which 8 were waited for; matrix products, arithmetic and copies ran while one was open for 2% of the time, Pallas kernels for 0%

profile of v1, /device:TPU:8, one launch (start us, length us, event | category | flops | bytes accessed | tf_op | source)
XLA Modules:
  0.0 1076.1 jit_solution(16485085148010052128)
XLA Ops:
  7.2 0.0 copy-start
  7.2 0.0 all-gather.5.cloned.1.call-start
  7.2 0.8 fusion.13
  8.0 1.5 broadcast_multiply_fusion
  9.6 0.0 all-gather.5.cloned.1.call-update
  9.6 0.0 all-gather.3.cloned.1.call-start
  9.6 1.5 broadcast_multiply_fusion.1
  11.2 0.0 all-gather.3.cloned.1.call-update
  11.2 0.0 all-reduce.14.cloned.1.call-start
  11.3 59.7 %all-gather.5.cloned.1.call-done = bf16[3072,512]{0,1:T(8,128)(2,1)} async-done(((bf16[3072,16]{0,1:T(8,128)(2,1)}), bf16[3072,512]{0,1:T(8,128)(2,1)}) %all-gather.5.cloned.1.call-update) | async-done | bytes 3145744 | tf_op jit(solution)/shard_map/all_gather | solution.py:60
  71.0 2.1 dynamic-slice_select_fusion
  73.2 55.8 %all-gather.3.cloned.1.call-done = bf16[3072,512]{0,1:T(8,128)(2,1)} async-done(((bf16[3072,16]{0,1:T(8,128)(2,1)}), bf16[3072,512]{0,1:T(8,128)(2,1)}) %all-gather.3.cloned.1.call-update) | async-done | bytes 3145744 | tf_op jit(solution)/shard_map/all_gather | solution.py:60
  129.0 2.1 dynamic-slice_select_fusion.1
  131.1 0.0 all-reduce.14.cloned.1.call-update
  131.2 0.0 reduce-scatter.3.cloned.1.call-start
  131.2 0.8 dynamic-slice_convert_fusion.2
  132.0 2.5 mul.55
  134.5 3.0 copy.18
  137.5 76.0 %all-reduce.14.cloned.1.call-done = (bf16[768,512]{0,1:T(8,128)(2,1)}, bf16[768,512]{0,1:T(8,128)(2,1)}) async-done(((bf16[768,512]{0,1:T(8,128)(2,1)}, bf16[768,512]{0,1:T(8,128)(2,1)}), (bf16[768,512]{0,1:T(8,128)(2,1)}, bf16[768,512]{0,1:T(8,128)(2,1)})) %all-reduce.14.cloned.1.call-update) | async-done | bytes 1572880 | tf_op jit(solution)/shard_map/psum | solution.py:11
  213.4 8.3 convolution_convert_fusion.1
  221.7 0.0 copy-start.7
  221.7 0.0 reduce-scatter.3.cloned.1.call-update
  221.8 0.0 all-reduce.12.cloned.1.call-start
  221.8 96.9 %reduce-scatter.3.cloned.1.call-done = bf16[96,512]{1,0:T(8,128)(2,1)} async-done(((bf16[3072,512]{1,0:T(8,128)(2,1)}), bf16[96,512]{1,0:T(8,128)(2,1)}) %reduce-scatter.3.cloned.1.call-update) | async-done | bytes 98320 | tf_op jit(solution)/shard_map/reduce_scatter | solution.py:64
  318.8 0.9 negate_convert_fusion
  319.7 0.0 copy-start.3
  319.7 2.3 fusion.11
  322.0 2.3 fusion.7
  324.3 0.0 all-reduce.12.cloned.1.call-update
  324.3 0.0 reduce-scatter.5.cloned.1.call-start
  324.4 0.0 copy-done.7
  324.4 8.0 convolution_convert_fusion
  332.3 0.0 copy-start.5
  332.3 0.0 copy-start.4
  332.3 0.0 reduce-scatter.5.cloned.1.call-update
  332.4 0.0 all-reduce.10.cloned.1.call-start
  332.4 76.3 %all-reduce.12.cloned.1.call-done = (f32[512,512]{1,0:T(8,128)}, f32[512,512]{1,0:T(8,128)}) async-done(((f32[512,512]{1,0:T(8,128)}, f32[512,512]{1,0:T(8,128)}), (f32[512,512]{1,0:T(8,128)}, f32[512,512]{1,0:T(8,128)})) %all-reduce.12.cloned.1.call-update) | async-done | bytes 2097168 | tf_op jit(solution)/shard_map/psum | solution.py:75
  408.7 0.0 all-reduce.10.cloned.1.call-update
  408.7 0.2 all-reduce.8.cloned.1.call-start
  409.0 100.7 %reduce-scatter.5.cloned.1.call-done = bf16[96,512]{1,0:T(8,128)(2,1)} async-done(((bf16[3072,512]{1,0:T(8,128)(2,1)}), bf16[96,512]{1,0:T(8,128)(2,1)}) %reduce-scatter.5.cloned.1.call-update) | async-done | bytes 98320 | tf_op jit(solution)/shard_map/reduce_scatter | solution.py:64
  509.7 0.0 copy-done.3
  509.7 0.0 copy-done
  509.7 1.1 fusion.6
  510.8 0.0 copy-start.6
  510.8 2.4 fusion.9
  513.2 0.0 all-reduce.8.cloned.1.call-update
  513.2 0.0 copy-done.5
  513.2 1.3 copy.14
  514.5 287.2 %all-reduce.10.cloned.1.call-done = (f32[512,512]{1,0:T(8,128)}, f32[512,512]{1,0:T(8,128)}) async-done(((f32[512,512]{1,0:T(8,128)}, f32[512,512]{1,0:T(8,128)}), (f32[512,512]{1,0:T(8,128)}, f32[512,512]{1,0:T(8,128)})) %all-reduce.10.cloned.1.call-update) | async-done | bytes 2097168 | tf_op jit(solution)/shard_map/psum | solution.py:74
  801.7 0.0 copy-done.4
  801.7 1.4 sub.18
  803.2 0.0 copy-start.1
  803.2 2.6 fusion.2
  805.8 0.0 copy-done.6
  805.8 0.0 copy-start.2
  805.8 257.4 %all-reduce.8.cloned.1.call-done = f32[512,512]{0,1:T(8,128)} async-done(((f32[512,512]{0,1:T(8,128)}), f32[512,512]{0,1:T(8,128)}) %all-reduce.8.cloned.1.call-update) | async-done | bytes 1048592 | tf_op jit(solution)/shard_map/psum | solution.py:90
  1063.2 3.5 fusion.4
  1066.8 2.5 copy.16
  1069.3 0.0 copy-done.1
  1069.3 0.0 copy-done.2
Async XLA Ops:
  7.2 502.5 %copy-start = (bf16[512,512]{1,0:T(8,128)(2,1)S(1)}, bf16[512,512]{1,0:T(8,128)(2,1)}, u32[]{:S(2)}) copy-start(bf16[512,512]{1,0:T(8,128)(2,1)} %param.15) | copy-start | bytes 1572868
  7.2 63.8 %all-gather.5.cloned.1.call-start = ((), (), s32[]{:S(2)}) async-start(), calls=%async_computation.4 | async-start | bytes 3244032 | tf_op jit(solution)/shard_map/all_gather | solution.py:60
  9.6 119.4 %all-gather.3.cloned.1.call-start = ((), (), s32[]{:S(2)}) async-start(), calls=%async_computation.2 | async-start | bytes 3244032 | tf_op jit(solution)/shard_map/all_gather | solution.py:60
  11.2 202.2 %all-reduce.14.cloned.1.call-start = ((), (), s32[]{:S(2)}) async-start(), calls=%async_computation.9 | async-start | bytes 3145728 | tf_op jit(solution)/shard_map/psum | solution.py:11
  131.2 187.6 %reduce-scatter.3.cloned.1.call-start = ((), (), s32[]{:S(2)}) async-start(), calls=%async_computation.3 | async-start | bytes 3244032 | tf_op jit(solution)/shard_map/reduce_scatter | solution.py:64
  221.7 102.6 %copy-start.7 = (bf16[768,512]{0,1:T(8,128)(2,1)S(1)}, bf16[768,512]{0,1:T(8,128)(2,1)}, u32[]{:S(2)}) copy-start(bf16[768,512]{0,1:T(8,128)(2,1)} %get-tuple-element.15) | copy-start | bytes 2359300
  221.8 187.0 %all-reduce.12.cloned.1.call-start = ((), (), s32[]{:S(2)}) async-start(), calls=%async_computation.8 | async-start | bytes 4194304 | tf_op jit(solution)/shard_map/psum | solution.py:75
  319.7 190.0 %copy-start.3 = (bf16[96,512]{1,0:T(8,128)(2,1)}, bf16[96,512]{1,0:T(8,128)(2,1)S(1)}, u32[]{:S(2)}) copy-start(bf16[96,512]{1,0:T(8,128)(2,1)S(1)} %negate_convert_fusion) | copy-start | bytes 294916
  324.3 185.4 %reduce-scatter.5.cloned.1.call-start = ((), (), s32[]{:S(2)}) async-start(), calls=%async_computation.5 | async-start | bytes 3244032 | tf_op jit(solution)/shard_map/reduce_scatter | solution.py:64
  332.3 180.9 %copy-start.5 = (f32[512,512]{1,0:T(8,128)S(1)}, f32[512,512]{1,0:T(8,128)}, u32[]{:S(2)}) copy-start(f32[512,512]{1,0:T(8,128)} %param.17) | copy-start | bytes 3145732
  332.3 469.4 %copy-start.4 = (f32[512,512]{1,0:T(8,128)S(1)}, f32[512,512]{1,0:T(8,128)}, u32[]{:S(2)}) copy-start(f32[512,512]{1,0:T(8,128)} %param.16) | copy-start | bytes 3145732
  332.4 469.4 %all-reduce.10.cloned.1.call-start = ((), (), s32[]{:S(2)}) async-start(), calls=%async_computation.7 | async-start | bytes 4194304 | tf_op jit(solution)/shard_map/psum | solution.py:74
  408.7 654.5 %all-reduce.8.cloned.1.call-start = ((), (), s32[]{:S(2)}) async-start(), calls=%async_computation.6 | async-start | bytes 2097152 | tf_op jit(solution)/shard_map/psum | solution.py:90
  510.8 295.0 %copy-start.6 = (bf16[96,512]{1,0:T(8,128)(2,1)}, bf16[96,512]{1,0:T(8,128)(2,1)S(1)}, u32[]{:S(2)}) copy-start(bf16[96,512]{1,0:T(8,128)(2,1)S(1)} %fusion.6) | copy-start | bytes 294916
  803.2 266.1 %copy-start.1 = (f32[512,512]{1,0:T(8,128)}, f32[512,512]{1,0:T(8,128)S(1)}, u32[]{:S(2)}) copy-start(f32[512,512]{1,0:T(8,128)S(1)} %sub.18) | copy-start | bytes 3145732
  805.8 263.5 %copy-start.2 = (f32[512,512]{1,0:T(8,128)}, f32[512,512]{1,0:T(8,128)S(1)}, u32[]{:S(2)}) copy-start(f32[512,512]{1,0:T(8,128)S(1)} %fusion.2) | copy-start | bytes 3145732
Sparse Core Ops, SparseCore 0:
  11.1 59.8 all-gather.4
  74.1 54.8 all-gather.2
  132.3 81.1 all-reduce.13
  221.9 96.8 reduce-scatter.2
  324.4 84.2 all-reduce.11
  413.0 96.6 reduce-scatter.4
  512.3 289.3 all-reduce.9
  808.6 254.5 all-reduce.7
